TPU v7x, 256 devices: a whole 4x4x8 slice. The times are simulated.
256 devices in a mesh: seq: 64 (over y, x_hi, z), head: 4 (over x_lo, core).
Axes of the slice: x: 4 (x_hi: 2, x_lo: 2; x = x_hi * 2 + x_lo), y: 4, z: 8, core: 2. Of those that a mesh axis runs over, the one named last changes fastest.
Arguments:
- qkv: bfloat16 [3, 49152, 1536], P(None, ('seq', 'head')), may hold values from -5 to 5
- key_tiles: int32 [12, 128, 27], P('head', 'seq'), may hold values from -1 to 127, as said below
Outputs:
- attended: bfloat16 [49152, 1536], P(('seq', 'head'))
Inputs may be any that keep to these rules, and one draw needn't show every extreme that they name: Each list key_tiles[n, g] names distinct tiles, the query tile g among them, each differing from g by at most 1 in the time tile, the tile row and the tile column; named tiles come first and -1 fills the rest of the list.
All inputs are finite; a program needn't handle non-finite values.
Results may differ from a plain program's by a relative error of at most 0.0035.
Values may be sent and summed in bfloat16 or wider, within the bound.
No kernel may reach another device: no remote copies, remote signals or barrier semaphores. Data moves between devices by JAX's collectives and lax.ppermute only.
A program may use at most 192 MiB of HBM per device.

v0:
```python
import jax
import jax.numpy as jnp
from jax import lax
from jax.sharding import PartitionSpec as P

TIME_TILES = 4
TILE_ROWS = 4


def from_behind(x, axis, by):
    length = lax.axis_size(axis)
    pairs = [(i, i + by) for i in range(length) if 0 <= i + by < length]
    return lax.ppermute(x, axis, pairs)


def swapped(value, axis, distance):
    mask = 2**distance
    pairs = [(source, source ^ mask) for source in range(lax.axis_size(axis))]
    return lax.ppermute(value, axis, pairs)


def attend(query_rows, keys, values, named_mask):
    blocks, slot_count, row_count, head_feature_width = keys.shape
    key_matrix_rows = keys.reshape(blocks, slot_count * row_count, head_feature_width)
    value_matrix_rows = values.reshape(blocks, slot_count * row_count, head_feature_width)
    logit_matrix = jnp.einsum(
        "jxg,jog->jxo", query_rows, key_matrix_rows, preferred_element_type=jnp.float32
    ) * head_feature_width ** (-0.5)
    score_mask = jnp.repeat(named_mask, row_count, axis=1)[:, None, :]
    logit_matrix = jnp.where(score_mask, logit_matrix, -jnp.inf)
    row_max = jnp.max(logit_matrix, axis=-1, keepdims=True)
    weights = jnp.exp(logit_matrix - row_max)
    row_total = jnp.sum(weights, axis=-1, keepdims=True)
    weighted_value_sum = jnp.einsum(
        "aop,ape->aoe",
        weights.astype(jnp.bfloat16),
        value_matrix_rows,
        preferred_element_type=jnp.float32,
    )
    return (weighted_value_sum / row_total).astype(jnp.bfloat16)


def pass_along(block, step_by):
    return from_behind(block, "seq", step_by)


def local(qkv, key_tiles):
    head_count = key_tiles.shape[0]
    col_count = lax.axis_size("seq") * 2 // (TIME_TILES * TILE_ROWS)
    time_stride = 1
    col_stride = 2 * TIME_TILES
    near_cols = 3
    seq_index = lax.axis_index("seq")
    own_time = seq_index % TIME_TILES
    own_pair = seq_index // TIME_TILES % 2
    own_col = seq_index // (2 * TIME_TILES)
    spread = lax.all_to_all(qkv, "head", split_axis=2, concat_axis=1, tiled=True)
    tile_tokens = spread.shape[1] // 2
    head_feature_width = spread.shape[2] // head_count
    query_rows = (
        spread[0].reshape(2, tile_tokens, head_count, head_feature_width).transpose(2, 0, 1, 3)
    )
    kv_pairs = (
        spread[1:3]
        .reshape(2, 2, tile_tokens, head_count, head_feature_width)
        .transpose(0, 3, 1, 2, 4)
    )
    side_bricks = [pass_along(kv_pairs, step_by) for step_by in (col_stride, -col_stride)]
    columns = jnp.stack([side_bricks[0], kv_pairs, side_bricks[1]], axis=2)
    edge_send = jnp.where(own_pair == 0, columns[:, :, :, 1], columns[:, :, :, 0])
    partner_rows = swapped(edge_send, "seq", 2)
    row_stack = jnp.concatenate(
        [partner_rows[:, :, :, None], columns, partner_rows[:, :, :, None]], axis=3
    )
    time_after, time_before = [
        pass_along(row_stack, step_by) for step_by in (-time_stride, time_stride)
    ]
    key_pool = jnp.stack([time_before, row_stack, time_after], axis=2)
    pool_size = 3 * near_cols * 4
    key_flat = key_pool[0].reshape(head_count * pool_size, tile_tokens, head_feature_width)
    value_flat = key_pool[1].reshape(head_count * pool_size, tile_tokens, head_feature_width)
    named_mask = key_tiles >= 0
    safe_tiles = jnp.where(named_mask, key_tiles, 0)
    tile_time = safe_tiles // 2 % TIME_TILES
    tile_row = safe_tiles // (2 * TIME_TILES) % 2 * 2 + safe_tiles % 2
    tile_col = safe_tiles // (4 * TIME_TILES)
    local_index = (
        ((tile_time - own_time + 1) * near_cols + tile_col - own_col + near_cols // 2) * 4
        + tile_row
        - 2 * own_pair
        + 1
    )
    head_base = (jnp.arange(head_count, dtype=jnp.int32) * pool_size)[:, None, None]
    pool_index = jnp.where(named_mask, local_index, 0) + head_base

    def full_block(operands):
        these_queries, these_index, these_named = operands
        return attend(these_queries, key_flat[these_index], value_flat[these_index], these_named)

    attended_tiles = lax.map(full_block, (query_rows, pool_index, named_mask))
    brick_out = attended_tiles.transpose(1, 2, 0, 3).reshape(
        2 * tile_tokens, head_count * head_feature_width
    )
    return lax.all_to_all(brick_out, "head", split_axis=0, concat_axis=1, tiled=True)


def solution(mesh):
    placed = (P(None, ("seq", "head"), None), P("head", "seq", None))
    return jax.shard_map(
        local, mesh=mesh, in_specs=placed, out_specs=P(("seq", "head"), None), check_vma=False
    )
```

profile of v0, /device:TPU:60, one launch (start us, length us, event | category | flops | bytes accessed | tf_op | source)
XLA Modules:
  0.0 656.3 jit_solution(152715509326859987)
XLA Ops:
  5.5 40.6 %all_to_all.34 = bf16[3,192,1536]{1,0,2:T(4,128)(2,1)S(1)} all-to-all(bf16[3,192,1536]{1,0,2:T(4,128)(2,1)} %copy.21), channel_id=1, replica_groups=mesh['seq'=64,'head'=4] {'head'}, dimensions={2} | all-to-all | bytes 3538944 | tf_op jit(solution)/shard_map/all_to_all | solution.py:57
  57.2 22.8 %collective-permute-done.1 = bf16[2,3,2,384,128]{4,3,2,1,0:T(8,128)(2,1)} collective-permute-done((bf16[2,3,2,384,128]{4,3,2,1,0:T(8,128)(2,1)}, bf16[2,3,2,384,128]{4,3,2,1,0:T(8,128)(2,1)}, u32[]{:S(2)}, u32[]{:S(2)}) %collective-permute-start.1) | collective-permute-done | bytes 1179680 | tf_op jit(solution)/shard_map/ppermute | solution.py:13
  82.3 26.7 %collective-permute-done = bf16[2,3,2,384,128]{4,3,2,1,0:T(8,128)(2,1)} collective-permute-done((bf16[2,3,2,384,128]{4,3,2,1,0:T(8,128)(2,1)}, bf16[2,3,2,384,128]{4,3,2,1,0:T(8,128)(2,1)}, u32[]{:S(2)}, u32[]{:S(2)}) %collective-permute-start) | collective-permute-done | bytes 1179680 | tf_op jit(solution)/shard_map/ppermute | solution.py:13
  116.9 6.4 collective-permute-start.2
  123.3 75.6 %collective-permute-done.2 = bf16[2,3,3,384,128]{4,3,2,1,0:T(8,128)(2,1)S(1)} collective-permute-done((bf16[2,3,3,384,128]{4,3,2,1,0:T(8,128)(2,1)S(1)}, bf16[2,3,3,384,128]{4,3,2,1,0:T(8,128)(2,1)S(1)}, u32[]{:S(2)}, u32[]{:S(2)}) %collective-permute-start.2) | collective-permute-done | bytes 1769504 | tf_op jit(solution)/shard_map/ppermute | solution.py:19
  201.9 9.4 %pad_maximum_fusion.1 = bf16[2,3,3,4,384,128]{5,1,4,3,0,2:T(4,128)(2,1)} fusion(bf16[2,3,3,1,384,128]{5,1,4,3,0,2:T(4,128)(2,1)S(1)} %bitcast.96, bf16[2,3,1,2,384,128]{5,1,4,3,0,2:T(4,128)(2,1)S(1)} %bitcast.91, bf16[2,3,1,2,384,128]{5,1,4,3,0,2:T(4,128)(2,1)S(1)} %bitcast.83, bf16[2,3,1,2,384,128]{5,1,4,3,0,2:T(4,128)(2,1)S(1)} %bitcast.94), kind=kLoop, calls=%fused_computation.24 | loop fusion | flops 14155776 | bytes 12386304 | tf_op jit(solution)/shard_map/concatenate | solution.py:72
  211.3 8.5 %copy.29 = bf16[2,3,3,4,384,128]{5,4,3,2,1,0:T(8,128)(2,1)} copy(bf16[2,3,3,4,384,128]{5,1,4,3,0,2:T(4,128)(2,1)} %pad_maximum_fusion.1) | data formatting | bytes 14155776 | tf_op jit(solution)/shard_map/concatenate | solution.py:72
  232.6 10.5 %fusion.37 = bf16[2,3,1,3,4,384,128]{6,1,5,4,0,3,2:T(4,128)(2,1)S(1)} fusion(bf16[2,3,3,1,384,128]{5,1,4,3,0,2:T(4,128)(2,1)} %bitcast.97, bf16[2,3,1,2,384,128]{5,1,4,3,0,2:T(4,128)(2,1)S(1)} %bitcast.92, bf16[2,3,1,2,384,128]{5,1,4,3,0,2:T(4,128)(2,1)S(1)} %bitcast.84, bf16[2,3,1,2,384,128]{5,1,4,3,0,2:T(4,128)(2,1)} %bitcast.95), kind=kLoop, calls=%fused_computation.63 | loop fusion | flops 14155776 | bytes 12386304 | tf_op jit(solution)/shard_map/stack | solution.py:78
  243.2 131.6 %collective-permute-done.4 = bf16[2,3,3,4,384,128]{5,4,3,2,1,0:T(8,128)(2,1)} collective-permute-done((bf16[2,3,3,4,384,128]{5,4,3,2,1,0:T(8,128)(2,1)}, bf16[2,3,3,4,384,128]{5,4,3,2,1,0:T(8,128)(2,1)}, u32[]{:S(2)}, u32[]{:S(2)}) %collective-permute-start.4) | collective-permute-done | bytes 7077920 | tf_op jit(solution)/shard_map/ppermute | solution.py:13
  374.7 10.3 %copy.45 = bf16[2,3,3,4,384,128]{5,1,4,3,0,2:T(4,128)(2,1)S(1)} copy(bf16[2,3,3,4,384,128]{5,4,3,2,1,0:T(8,128)(2,1)} %collective-permute-done.4) | data formatting | bytes 14155776 | tf_op jit(solution)/shard_map/ppermute | solution.py:13
  385.1 11.0 %copy.46 = bf16[2,3,3,4,384,128]{5,1,4,3,0,2:T(4,128)(2,1)} copy(bf16[2,3,3,4,384,128]{5,4,3,2,1,0:T(8,128)(2,1)} %collective-permute-done.3) | data formatting | bytes 14155776 | tf_op jit(solution)/shard_map/ppermute | solution.py:13
  396.1 27.2 %pad_maximum_fusion = bf16[2,3,3,3,4,384,128]{6,1,5,4,0,3,2:T(4,128)(2,1)} fusion(bf16[2,3,1,3,4,384,128]{6,1,5,4,0,3,2:T(4,128)(2,1)S(1)} %bitcast.85, bf16[2,3,1,3,4,384,128]{6,1,5,4,0,3,2:T(4,128)(2,1)S(1)} %fusion.37, bf16[2,3,1,3,4,384,128]{6,1,5,4,0,3,2:T(4,128)(2,1)} %bitcast.86), kind=kLoop, calls=%fused_computation.23 | loop fusion | flops 21233664 | bytes 42467328 | tf_op jit(solution)/shard_map/stack | solution.py:78
  423.3 19.9 %fusion.34 = (bf16[1,3,3,3,4,384,128]{6,1,5,4,0,3,2:T(4,128)(2,1)}, bf16[1,3,3,3,4,384,128]{6,1,5,4,0,3,2:T(4,128)(2,1)}) fusion(bf16[2,3,3,3,4,384,128]{6,1,5,4,0,3,2:T(4,128)(2,1)} %pad_maximum_fusion), kind=kLoop, calls=%fused_computation.62 | loop fusion | bytes 42467328 | tf_op jit(solution)/shard_map/slice | solution.py:81
  443.2 12.1 %copy.33 = bf16[1,3,3,3,4,384,128]{6,5,4,3,2,1,0:T(8,128)(2,1)} copy(bf16[1,3,3,3,4,384,128]{6,1,5,4,0,3,2:T(4,128)(2,1)} %get-tuple-element.81) | data formatting | bytes 21233664 | tf_op jit(solution)/shard_map/slice | solution.py:80
  456.3 5.7 copy.34
  462.0 180.4 %while.10 = (s32[]{:T(128)}, bf16[3,2,384,128]{3,2,1,0:T(8,128)(2,1)S(1)}, pred[3,2,27]{2,1,0:T(4,128)(4,1)S(1)}, bf16[3,2,384,128]{3,2,1,0:T(8,128)(2,1)}, s32[...) while((s32[]{:T(128)}, ...), condition=%wide.region_3.4_spmd, body=%wide.region_0.3_spmd.sunk | while | flops 4164648448 | bytes 127962088 | solution.py:100
  462.1 7.7 %gather_fusion.1 = bf16[54,384,128]{2,1,0:T(8,128)(2,1)} fusion(bf16[108,384,128]{2,1,0:T(8,128)(2,1)} %get-tuple-element.150, s32[1024]{0:T(1024)S(1)} %pad_clamp_fusion.2), kind=kCustom, calls=%fused_computation.clone.1 | custom fusion | bytes 10617048 | tf_op jit(solution)/shard_map/while/body/eval_jaxpr/gather | solution.py:98
  469.9 14.9 %fusion.47 = (f32[2,384]{1,0:T(2,128)S(1)}, f32[2,384,10368]{2,1,0:T(8,128)}) fusion(pred[2,10368]{1,0:T(4,128)(4,1)S(1)} %bitcast.87, bf16[2,10368,128]{2,1,0:T(8,128)(2,1)} %bitcast.77, bf16[3,2,384,128]{3,2,1,0:T(8,128)(2,1)} %get-tuple-element.148, s32[]{:T(128)} %get-tuple-element.137), kind=kOutput, calls=%fused_computation.4.clone.1 | convolution fusion | flops 2062318848 | bytes 37379840 | tf_op jit(solution)/shard_map/while/body/eval_jaxpr/jxg,jog->jxo/dot_general | solution.py:26
  484.7 14.3 %fusion.48 = f32[2,384]{1,0:T(2,128)S(1)} fusion(f32[2,384,10368]{2,1,0:T(8,128)} %get-tuple-element.127, f32[2,384]{1,0:T(2,128)S(1)} %get-tuple-element.128, pred[2,10368]{1,0:T(4,128)(4,1)S(1)} %bitcast.88), kind=kLoop, calls=%fused_computation.5.clone.1 | loop fusion | flops 31849728 | bytes 31877376 | tf_op jit(solution)/shard_map/while/body/eval_jaxpr/reduce_sum | solution.py:33
  499.0 7.7 %gather_fusion = bf16[54,384,128]{2,1,0:T(8,128)(2,1)} fusion(bf16[108,384,128]{2,1,0:T(8,128)(2,1)} %get-tuple-element.151, s32[1024]{0:T(1024)S(1)} %pad_clamp_fusion.2), kind=kCustom, calls=%fused_computation.1.clone.1 | custom fusion | bytes 10617048 | tf_op jit(solution)/shard_map/while/body/eval_jaxpr/gather | solution.py:98
  506.7 15.4 %fusion.49 = bf16[3,2,384,128]{3,2,1,0:T(8,128)(2,1)S(1)} fusion(bf16[3,2,384,128]{3,2,1,0:T(8,128)(2,1)S(1)} %get-tuple-element.138, s32[]{:T(128)} %get-tuple-element.137, bf16[2,10368,128]{2,1,0:T(8,128)(2,1)} %bitcast.78, f32[2,384,10368]{2,1,0:T(8,128)} %get-tuple-element.127, f32[2,384]{1,0:T(2,128)S(1)} %get-tuple-element.128, ...), kind=kOutput, calls=%fused_computation.12.clone.1 | convolution fusion | flops 2070478848 | bytes 37403140 | tf_op jit(solution)/shard_map/while/body/eval_jaxpr/aop,ape->aoe/dot_general | solution.py:34
  522.2 7.7 %gather_fusion.1 = bf16[54,384,128]{2,1,0:T(8,128)(2,1)} fusion(bf16[108,384,128]{2,1,0:T(8,128)(2,1)} %get-tuple-element.150, s32[1024]{0:T(1024)S(1)} %pad_clamp_fusion.2), kind=kCustom, calls=%fused_computation.clone.1 | custom fusion | bytes 10617048 | tf_op jit(solution)/shard_map/while/body/eval_jaxpr/gather | solution.py:98
  530.0 14.9 %fusion.47 = (f32[2,384]{1,0:T(2,128)S(1)}, f32[2,384,10368]{2,1,0:T(8,128)}) fusion(pred[2,10368]{1,0:T(4,128)(4,1)S(1)} %bitcast.87, bf16[2,10368,128]{2,1,0:T(8,128)(2,1)} %bitcast.77, bf16[3,2,384,128]{3,2,1,0:T(8,128)(2,1)} %get-tuple-element.148, s32[]{:T(128)} %get-tuple-element.137), kind=kOutput, calls=%fused_computation.4.clone.1 | convolution fusion | flops 2062318848 | bytes 37379840 | tf_op jit(solution)/shard_map/while/body/eval_jaxpr/jxg,jog->jxo/dot_general | solution.py:26
  544.9 14.3 %fusion.48 = f32[2,384]{1,0:T(2,128)S(1)} fusion(f32[2,384,10368]{2,1,0:T(8,128)} %get-tuple-element.127, f32[2,384]{1,0:T(2,128)S(1)} %get-tuple-element.128, pred[2,10368]{1,0:T(4,128)(4,1)S(1)} %bitcast.88), kind=kLoop, calls=%fused_computation.5.clone.1 | loop fusion | flops 31849728 | bytes 31877376 | tf_op jit(solution)/shard_map/while/body/eval_jaxpr/reduce_sum | solution.py:33
  559.2 7.7 %gather_fusion = bf16[54,384,128]{2,1,0:T(8,128)(2,1)} fusion(bf16[108,384,128]{2,1,0:T(8,128)(2,1)} %get-tuple-element.151, s32[1024]{0:T(1024)S(1)} %pad_clamp_fusion.2), kind=kCustom, calls=%fused_computation.1.clone.1 | custom fusion | bytes 10617048 | tf_op jit(solution)/shard_map/while/body/eval_jaxpr/gather | solution.py:98
  566.8 15.4 %fusion.49 = bf16[3,2,384,128]{3,2,1,0:T(8,128)(2,1)S(1)} fusion(bf16[3,2,384,128]{3,2,1,0:T(8,128)(2,1)S(1)} %get-tuple-element.138, s32[]{:T(128)} %get-tuple-element.137, bf16[2,10368,128]{2,1,0:T(8,128)(2,1)} %bitcast.78, f32[2,384,10368]{2,1,0:T(8,128)} %get-tuple-element.127, f32[2,384]{1,0:T(2,128)S(1)} %get-tuple-element.128, ...), kind=kOutput, calls=%fused_computation.12.clone.1 | convolution fusion | flops 2070478848 | bytes 37403140 | tf_op jit(solution)/shard_map/while/body/eval_jaxpr/aop,ape->aoe/dot_general | solution.py:34
  582.4 7.7 %gather_fusion.1 = bf16[54,384,128]{2,1,0:T(8,128)(2,1)} fusion(bf16[108,384,128]{2,1,0:T(8,128)(2,1)} %get-tuple-element.150, s32[1024]{0:T(1024)S(1)} %pad_clamp_fusion.2), kind=kCustom, calls=%fused_computation.clone.1 | custom fusion | bytes 10617048 | tf_op jit(solution)/shard_map/while/body/eval_jaxpr/gather | solution.py:98
  590.2 14.9 %fusion.47 = (f32[2,384]{1,0:T(2,128)S(1)}, f32[2,384,10368]{2,1,0:T(8,128)}) fusion(pred[2,10368]{1,0:T(4,128)(4,1)S(1)} %bitcast.87, bf16[2,10368,128]{2,1,0:T(8,128)(2,1)} %bitcast.77, bf16[3,2,384,128]{3,2,1,0:T(8,128)(2,1)} %get-tuple-element.148, s32[]{:T(128)} %get-tuple-element.137), kind=kOutput, calls=%fused_computation.4.clone.1 | convolution fusion | flops 2062318848 | bytes 37379840 | tf_op jit(solution)/shard_map/while/body/eval_jaxpr/jxg,jog->jxo/dot_general | solution.py:26
  605.0 14.3 %fusion.48 = f32[2,384]{1,0:T(2,128)S(1)} fusion(f32[2,384,10368]{2,1,0:T(8,128)} %get-tuple-element.127, f32[2,384]{1,0:T(2,128)S(1)} %get-tuple-element.128, pred[2,10368]{1,0:T(4,128)(4,1)S(1)} %bitcast.88), kind=kLoop, calls=%fused_computation.5.clone.1 | loop fusion | flops 31849728 | bytes 31877376 | tf_op jit(solution)/shard_map/while/body/eval_jaxpr/reduce_sum | solution.py:33
  619.3 7.7 %gather_fusion = bf16[54,384,128]{2,1,0:T(8,128)(2,1)} fusion(bf16[108,384,128]{2,1,0:T(8,128)(2,1)} %get-tuple-element.151, s32[1024]{0:T(1024)S(1)} %pad_clamp_fusion.2), kind=kCustom, calls=%fused_computation.1.clone.1 | custom fusion | bytes 10617048 | tf_op jit(solution)/shard_map/while/body/eval_jaxpr/gather | solution.py:98
  627.0 15.4 %fusion.49 = bf16[3,2,384,128]{3,2,1,0:T(8,128)(2,1)S(1)} fusion(bf16[3,2,384,128]{3,2,1,0:T(8,128)(2,1)S(1)} %get-tuple-element.138, s32[]{:T(128)} %get-tuple-element.137, bf16[2,10368,128]{2,1,0:T(8,128)(2,1)} %bitcast.78, f32[2,384,10368]{2,1,0:T(8,128)} %get-tuple-element.127, f32[2,384]{1,0:T(2,128)S(1)} %get-tuple-element.128, ...), kind=kOutput, calls=%fused_computation.12.clone.1 | convolution fusion | flops 2070478848 | bytes 37403140 | tf_op jit(solution)/shard_map/while/body/eval_jaxpr/aop,ape->aoe/dot_general | solution.py:34
  643.5 11.9 %all_to_all.35 = bf16[4,192,384]{2,1,0:T(8,128)(2,1)S(1)} all-to-all(bf16[4,192,384]{2,1,0:T(8,128)(2,1)S(1)} %all_to_all.28), channel_id=1, replica_groups=mesh['seq'=64,'head'=4] {'head'}, dimensions={0} | all-to-all | bytes 1179648 | tf_op jit(solution)/shard_map/all_to_all | solution.py:104
  (54 shorter events, 46.0 us)
Async XLA Ops:
  52.5 27.6 %collective-permute-start.1 = (bf16[2,3,2,384,128]{4,3,2,1,0:T(8,128)(2,1)}, bf16[2,3,2,384,128]{4,3,2,1,0:T(8,128)(2,1)}, u32[]{:S(2)}, u32[]{:S(2)}) collective-permute-start(bf16[2,3,2,384,128]{4,3,2,1,0:T(8,128)(2,1)} %copy.23), channel_id=1, source_target_pairs={{32,0},{36,4},{40,8},{44,12},{48,16},{52,20},{56,24},{60,28},{64,3... | collective-permute-start | bytes 3538952 | tf_op jit(solution)/shard_map/ppermute | solution.py:13
  55.9 53.1 %collective-permute-start = (bf16[2,3,2,384,128]{4,3,2,1,0:T(8,128)(2,1)}, bf16[2,3,2,384,128]{4,3,2,1,0:T(8,128)(2,1)}, u32[]{:S(2)}, u32[]{:S(2)}) collective-permute-start(bf16[2,3,2,384,128]{4,3,2,1,0:T(8,128)(2,1)} %copy.23), channel_id=1, source_target_pairs={{0,32},{4,36},{8,40},{12,44},{16,48},{20,52},{24,56},{28,60},{32,6... | collective-permute-start | bytes 3538952 | tf_op jit(solution)/shard_map/ppermute | solution.py:13
  111.3 89.2 %copy-start.1 = (bf16[2,3,2,384,128]{4,1,3,2,0:T(4,128)(2,1)}, bf16[2,3,2,384,128]{4,1,3,2,0:T(4,128)(2,1)S(1)}, u32[]{:S(2)}) copy-start(bf16[2,3,2,384,128]{4,1,3,2,0:T(4,128)(2,1)S(1)} %copy.49) | copy-start | bytes 3538948
  116.9 82.0 %collective-permute-start.2 = (bf16[2,3,3,384,128]{4,3,2,1,0:T(8,128)(2,1)S(1)}, bf16[2,3,3,384,128]{4,3,2,1,0:T(8,128)(2,1)S(1)}, u32[]{:S(2)}, u32[]{:S(2)}) collective-permute-start(bf16[2,3,3,384,128]{4,3,2,1,0:T(8,128)(2,1)S(1)} %copy.27), channel_id=1, source_target_pairs={{0,16},{4,20},{8,24},{12,28},{16,0},{20,4},{24,8},{28,12},{32,48},... | collective-permute-start | bytes 5308424 | tf_op jit(solution)/shard_map/ppermute | solution.py:19
  200.5 1.5 copy-start.2
  211.3 14.6 %copy-start.4 = (s32[3,2,27]{2,1,0:T(2,128)S(1)}, s32[3,2,27]{2,1,0:T(2,128)}, u32[]{:S(2)}) copy-start(s32[3,2,27]{2,1,0:T(2,128)} %param.5) | copy-start | bytes 1948
  219.8 154.9 %collective-permute-start.4 = (bf16[2,3,3,4,384,128]{5,4,3,2,1,0:T(8,128)(2,1)}, bf16[2,3,3,4,384,128]{5,4,3,2,1,0:T(8,128)(2,1)}, u32[]{:S(2)}, u32[]{:S(2)}) collective-permute-start(bf16[2,3,3,4,384,128]{5,4,3,2,1,0:T(8,128)(2,1)} %copy.29), channel_id=1, source_target_pairs={{4,0},{8,4},{12,8},{16,12},{20,16},{24,20},{28,24},{32,28},{36,32}... | collective-permute-start | bytes 21233672 | tf_op jit(solution)/shard_map/ppermute | solution.py:13
  221.7 163.3 %collective-permute-start.3 = (bf16[2,3,3,4,384,128]{5,4,3,2,1,0:T(8,128)(2,1)}, bf16[2,3,3,4,384,128]{5,4,3,2,1,0:T(8,128)(2,1)}, u32[]{:S(2)}, u32[]{:S(2)}) collective-permute-start(bf16[2,3,3,4,384,128]{5,4,3,2,1,0:T(8,128)(2,1)} %copy.29), channel_id=1, source_target_pairs={{0,4},{4,8},{8,12},{12,16},{16,20},{20,24},{24,28},{28,32},{32,36}... | collective-permute-start | bytes 21233672 | tf_op jit(solution)/shard_map/ppermute | solution.py:13
  443.2 13.1 %copy-start = (bf16[1,3,3,3,4,384,128]{6,1,5,4,0,3,2:T(4,128)(2,1)S(1)}, bf16[1,3,3,3,4,384,128]{6,1,5,4,0,3,2:T(4,128)(2,1)}, u32[]{:S(2)}) copy-start(bf16[1,3,3,3,4,384,128]{6,1,5,4,0,3,2:T(4,128)(2,1)} %get-tuple-element.80) | copy-start | bytes 31850500
  456.3 5.7 copy-start.3
where the time goes:
time: 658 us; the launch traced here: 656 us
  waiting for transfers between devices  257 us (39%)
  local copies, waits for them, and re-layouts  143 us (22%)
  other arithmetic  95.3 us (14%)
  matrix products  90.9 us (14%)
  blocking collectives  52.5 us (8%)
  starting transfers between devices  17.1 us (3%)
    ppermute x4, waiting for transfers between devices, from_behind(): return lax.ppermute(x, axis, pairs)  181 us
    ppermute x1, waiting for transfers between devices, swapped(): return lax.ppermute(value, axis, pairs)  75.6 us
    dot_general x3, matrix products, attend(): jnp.einsum('aop,ape->aoe', weights.astype(jnp.bfloat16), value_matrix_row...  46.3 us
    dot_general x3, matrix products, attend(): jnp.einsum('jxg,jog->jxo', query_rows, key_matrix_rows, preferred_element...  44.6 us
    reduce_sum x3, other arithmetic, attend(): row_total = jnp.sum(weights, axis=-1, keepdims=True)  42.8 us
    all_to_all x1, blocking collectives, local(): lax.all_to_all(qkv, 'head', split_axis=2, concat_axis=1, tiled=True)  40.6 us
    another operation x2, other arithmetic, local(): key_pool = jnp.stack([time_before, row_stack, time_after], axis=2)  37.7 us
    ppermute x4, local copies, waits for them, and re-layouts, from_behind(): return lax.ppermute(x, axis, pairs)  25.9 us
  transfers between devices with their start and end apart: 5, of which 4 were waited for; matrix products, arithmetic and copies ran while one was open for 5% of the time, Pallas kernels for 0%

commit v1 on v0

--- a/solution.py
+++ b/solution.py
@@ -54,7 +54,12 @@
     own_time = seq_index % TIME_TILES
     own_pair = seq_index // TIME_TILES % 2
     own_col = seq_index // (2 * TIME_TILES)
-    spread = lax.all_to_all(qkv, "head", split_axis=2, concat_axis=1, tiled=True)
+    spread = jnp.concatenate(
+        jax.lax.all_to_all(
+            jnp.stack(jnp.split(qkv, jax.lax.psum(1, "head"), 2), axis=0), "head", 0, 0
+        ),
+        1,
+    )
     tile_tokens = spread.shape[1] // 2
     head_feature_width = spread.shape[2] // head_count
     query_rows = (

time: 658 us -> 635 us (0.965)
  blocking collectives: 52.5 us -> 36.6 us
  local copies, waits for them, and re-layouts: 143 us -> 136 us
    all_to_all x1, blocking collectives: 40.6 us -> 24.6 us  [local(): jax.lax.all_to_all(jnp.stack(jnp.split(qkv, jax.lax.psum(1, 'head'), 2),...]
where the time goes in v1:
time: 635 us; the launch traced here: 634 us
  waiting for transfers between devices  257 us (40%)
  local copies, waits for them, and re-layouts  136 us (21%)
  other arithmetic  95.6 us (15%)
  matrix products  90.7 us (14%)
  blocking collectives  36.6 us (6%)
  starting transfers between devices  17.2 us (3%)
    ppermute x4, waiting for transfers between devices, from_behind(): return lax.ppermute(x, axis, pairs)  181 us
    ppermute x1, waiting for transfers between devices, swapped(): return lax.ppermute(value, axis, pairs)  76 us
    dot_general x3, matrix products, attend(): jnp.einsum('aop,ape->aoe', weights.astype(jnp.bfloat16), value_matrix_row...  46.3 us
    dot_general x3, matrix products, attend(): jnp.einsum('jxg,jog->jxo', query_rows, key_matrix_rows, preferred_element...  44.4 us
    reduce_sum x3, other arithmetic, attend(): row_total = jnp.sum(weights, axis=-1, keepdims=True)  42.8 us
    another operation x2, other arithmetic, local(): key_pool = jnp.stack([time_before, row_stack, time_after], axis=2)  37.8 us
    ppermute x4, local copies, waits for them, and re-layouts, from_behind(): return lax.ppermute(x, axis, pairs)  25.9 us
    slice x2, local copies, waits for them, and re-layouts, local(): key_pool[1].reshape(head_count * pool_size, tile_tokens, head_feature_width)  25.7 us
  transfers between devices with their start and end apart: 5, of which 4 were waited for; matrix products, arithmetic and copies ran while one was open for 5% of the time, Pallas kernels for 0%

profile of v1, /device:TPU:60, one launch (start us, length us, event | category | flops | bytes accessed | tf_op | source)
XLA Modules:
  0.0 634.0 jit_solution(10203485765463250554)
XLA Ops:
  1.9 24.6 %all_to_all.24 = bf16[4,3,192,384]{3,2,1,0:T(8,128)(2,1)S(1)} all-to-all(bf16[4,3,192,384]{3,2,1,0:T(8,128)(2,1)S(1)} %pad_maximum_fusion.3), channel_id=1, replica_groups=mesh['seq'=64,'head'=4] {'head'}, dimensions={0} | all-to-all | bytes 3538944 | tf_op jit(solution)/shard_map/all_to_all | solution.py:58
  34.4 23.1 %collective-permute-done.1 = bf16[2,3,2,384,128]{4,3,2,1,0:T(8,128)(2,1)} collective-permute-done((bf16[2,3,2,384,128]{4,3,2,1,0:T(8,128)(2,1)}, bf16[2,3,2,384,128]{4,3,2,1,0:T(8,128)(2,1)}, u32[]{:S(2)}, u32[]{:S(2)}) %collective-permute-start.1) | collective-permute-done | bytes 1179680 | tf_op jit(solution)/shard_map/ppermute | solution.py:13
  59.8 26.5 %collective-permute-done = bf16[2,3,2,384,128]{4,3,2,1,0:T(8,128)(2,1)} collective-permute-done((bf16[2,3,2,384,128]{4,3,2,1,0:T(8,128)(2,1)}, bf16[2,3,2,384,128]{4,3,2,1,0:T(8,128)(2,1)}, u32[]{:S(2)}, u32[]{:S(2)}) %collective-permute-start) | collective-permute-done | bytes 1179680 | tf_op jit(solution)/shard_map/ppermute | solution.py:13
  94.2 6.4 %collective-permute-start.2 = (bf16[2,3,3,384,128]{4,3,2,1,0:T(8,128)(2,1)S(1)}, bf16[2,3,3,384,128]{4,3,2,1,0:T(8,128)(2,1)S(1)}, u32[]{:S(2)}, u32[]{:S(2)}) collective-permute-start(bf16[2,3,3,384,128]{4,3,2,1,0:T(8,128)(2,1)S(1)} %copy.26), channel_id=1, source_target_pairs={{0,16},{4,20},{8,24},{12,28},{16,0},{20,4},{24,8},{28,12},{32,48},... | collective-permute-start | bytes 5308424 | tf_op jit(solution)/shard_map/ppermute | solution.py:19
  100.6 76.0 %collective-permute-done.2 = bf16[2,3,3,384,128]{4,3,2,1,0:T(8,128)(2,1)S(1)} collective-permute-done((bf16[2,3,3,384,128]{4,3,2,1,0:T(8,128)(2,1)S(1)}, bf16[2,3,3,384,128]{4,3,2,1,0:T(8,128)(2,1)S(1)}, u32[]{:S(2)}, u32[]{:S(2)}) %collective-permute-start.2) | collective-permute-done | bytes 1769504 | tf_op jit(solution)/shard_map/ppermute | solution.py:19
  179.6 9.4 %pad_maximum_fusion.1 = bf16[2,3,3,4,384,128]{5,1,4,3,0,2:T(4,128)(2,1)} fusion(bf16[2,3,3,1,384,128]{5,1,4,3,0,2:T(4,128)(2,1)S(1)} %bitcast.105, bf16[2,3,1,2,384,128]{5,1,4,3,0,2:T(4,128)(2,1)S(1)} %bitcast.100, bf16[2,3,1,2,384,128]{5,1,4,3,0,2:T(4,128)(2,1)S(1)} %bitcast.92, bf16[2,3,1,2,384,128]{5,1,4,3,0,2:T(4,128)(2,1)S(1)} %bitcast.103), kind=kLoop, calls=%fused_computation.24 | loop fusion | flops 14155776 | bytes 12386304 | tf_op jit(solution)/shard_map/concatenate | solution.py:77
  189.0 8.5 %copy.28 = bf16[2,3,3,4,384,128]{5,4,3,2,1,0:T(8,128)(2,1)} copy(bf16[2,3,3,4,384,128]{5,1,4,3,0,2:T(4,128)(2,1)} %pad_maximum_fusion.1) | data formatting | bytes 14155776 | tf_op jit(solution)/shard_map/concatenate | solution.py:77
  210.3 10.5 %fusion.37 = bf16[2,3,1,3,4,384,128]{6,1,5,4,0,3,2:T(4,128)(2,1)S(1)} fusion(bf16[2,3,3,1,384,128]{5,1,4,3,0,2:T(4,128)(2,1)} %bitcast.106, bf16[2,3,1,2,384,128]{5,1,4,3,0,2:T(4,128)(2,1)S(1)} %bitcast.101, bf16[2,3,1,2,384,128]{5,1,4,3,0,2:T(4,128)(2,1)S(1)} %bitcast.93, bf16[2,3,1,2,384,128]{5,1,4,3,0,2:T(4,128)(2,1)} %bitcast.104), kind=kLoop, calls=%fused_computation.68 | loop fusion | flops 14155776 | bytes 12386304 | tf_op jit(solution)/shard_map/stack | solution.py:83
  220.8 131.6 %collective-permute-done.4 = bf16[2,3,3,4,384,128]{5,4,3,2,1,0:T(8,128)(2,1)} collective-permute-done((bf16[2,3,3,4,384,128]{5,4,3,2,1,0:T(8,128)(2,1)}, bf16[2,3,3,4,384,128]{5,4,3,2,1,0:T(8,128)(2,1)}, u32[]{:S(2)}, u32[]{:S(2)}) %collective-permute-start.4) | collective-permute-done | bytes 7077920 | tf_op jit(solution)/shard_map/ppermute | solution.py:13
  352.4 10.3 %copy.44 = bf16[2,3,3,4,384,128]{5,1,4,3,0,2:T(4,128)(2,1)S(1)} copy(bf16[2,3,3,4,384,128]{5,4,3,2,1,0:T(8,128)(2,1)} %collective-permute-done.4) | data formatting | bytes 14155776 | tf_op jit(solution)/shard_map/ppermute | solution.py:13
  362.7 11.1 %copy.45 = bf16[2,3,3,4,384,128]{5,1,4,3,0,2:T(4,128)(2,1)} copy(bf16[2,3,3,4,384,128]{5,4,3,2,1,0:T(8,128)(2,1)} %collective-permute-done.3) | data formatting | bytes 14155776 | tf_op jit(solution)/shard_map/ppermute | solution.py:13
  373.8 27.2 %pad_maximum_fusion = bf16[2,3,3,3,4,384,128]{6,1,5,4,0,3,2:T(4,128)(2,1)} fusion(bf16[2,3,1,3,4,384,128]{6,1,5,4,0,3,2:T(4,128)(2,1)S(1)} %bitcast.94, bf16[2,3,1,3,4,384,128]{6,1,5,4,0,3,2:T(4,128)(2,1)S(1)} %fusion.37, bf16[2,3,1,3,4,384,128]{6,1,5,4,0,3,2:T(4,128)(2,1)} %bitcast.95), kind=kLoop, calls=%fused_computation.23 | loop fusion | flops 21233664 | bytes 42467328 | tf_op jit(solution)/shard_map/stack | solution.py:83
  401.0 19.9 %fusion.34 = (bf16[1,3,3,3,4,384,128]{6,1,5,4,0,3,2:T(4,128)(2,1)}, bf16[1,3,3,3,4,384,128]{6,1,5,4,0,3,2:T(4,128)(2,1)}) fusion(bf16[2,3,3,3,4,384,128]{6,1,5,4,0,3,2:T(4,128)(2,1)} %pad_maximum_fusion), kind=kLoop, calls=%fused_computation.67 | loop fusion | bytes 42467328 | tf_op jit(solution)/shard_map/slice | solution.py:86
  420.9 12.1 %copy.32 = bf16[1,3,3,3,4,384,128]{6,5,4,3,2,1,0:T(8,128)(2,1)} copy(bf16[1,3,3,3,4,384,128]{6,1,5,4,0,3,2:T(4,128)(2,1)} %get-tuple-element.81) | data formatting | bytes 21233664 | tf_op jit(solution)/shard_map/slice | solution.py:85
  434.0 5.8 copy.33
  439.8 180.3 %while.10 = (s32[]{:T(128)}, bf16[3,2,384,128]{3,2,1,0:T(8,128)(2,1)S(1)}, pred[3,2,27]{2,1,0:T(4,128)(4,1)S(1)}, bf16[3,2,384,128]{3,2,1,0:T(8,128)(2,1)}, s32[...) while((s32[]{:T(128)}, ...), condition=%wide.region_3.4_spmd, body=%wide.region_0.3_spmd.sunk | while | flops 4164648448 | bytes 127962088 | solution.py:105
  439.9 7.7 %gather_fusion.1 = bf16[54,384,128]{2,1,0:T(8,128)(2,1)} fusion(bf16[108,384,128]{2,1,0:T(8,128)(2,1)} %get-tuple-element.154, s32[1024]{0:T(1024)S(1)} %pad_clamp_fusion.2), kind=kCustom, calls=%fused_computation.clone.1 | custom fusion | bytes 10617048 | tf_op jit(solution)/shard_map/while/body/eval_jaxpr/gather | solution.py:103
  447.7 14.8 %fusion.47 = (f32[2,384]{1,0:T(2,128)S(1)}, f32[2,384,10368]{2,1,0:T(8,128)}) fusion(pred[2,10368]{1,0:T(4,128)(4,1)S(1)} %bitcast.96, bf16[2,10368,128]{2,1,0:T(8,128)(2,1)} %bitcast.86, bf16[3,2,384,128]{3,2,1,0:T(8,128)(2,1)} %get-tuple-element.152, s32[]{:T(128)} %get-tuple-element.141), kind=kOutput, calls=%fused_computation.4.clone.1 | convolution fusion | flops 2062318848 | bytes 37379840 | tf_op jit(solution)/shard_map/while/body/eval_jaxpr/jxg,jog->jxo/dot_general | solution.py:26
  462.5 14.3 %fusion.48 = f32[2,384]{1,0:T(2,128)S(1)} fusion(f32[2,384,10368]{2,1,0:T(8,128)} %get-tuple-element.131, f32[2,384]{1,0:T(2,128)S(1)} %get-tuple-element.132, pred[2,10368]{1,0:T(4,128)(4,1)S(1)} %bitcast.97), kind=kLoop, calls=%fused_computation.5.clone.1 | loop fusion | flops 31849728 | bytes 31877376 | tf_op jit(solution)/shard_map/while/body/eval_jaxpr/reduce_sum | solution.py:33
  476.8 7.7 %gather_fusion = bf16[54,384,128]{2,1,0:T(8,128)(2,1)} fusion(bf16[108,384,128]{2,1,0:T(8,128)(2,1)} %get-tuple-element.155, s32[1024]{0:T(1024)S(1)} %pad_clamp_fusion.2), kind=kCustom, calls=%fused_computation.1.clone.1 | custom fusion | bytes 10617048 | tf_op jit(solution)/shard_map/while/body/eval_jaxpr/gather | solution.py:103
  484.5 15.4 %fusion.49 = bf16[3,2,384,128]{3,2,1,0:T(8,128)(2,1)S(1)} fusion(bf16[3,2,384,128]{3,2,1,0:T(8,128)(2,1)S(1)} %get-tuple-element.142, s32[]{:T(128)} %get-tuple-element.141, bf16[2,10368,128]{2,1,0:T(8,128)(2,1)} %bitcast.87, f32[2,384,10368]{2,1,0:T(8,128)} %get-tuple-element.131, f32[2,384]{1,0:T(2,128)S(1)} %get-tuple-element.132, ...), kind=kOutput, calls=%fused_computation.12.clone.1 | convolution fusion | flops 2070478848 | bytes 37403140 | tf_op jit(solution)/shard_map/while/body/eval_jaxpr/aop,ape->aoe/dot_general | solution.py:34
  500.0 7.7 %gather_fusion.1 = bf16[54,384,128]{2,1,0:T(8,128)(2,1)} fusion(bf16[108,384,128]{2,1,0:T(8,128)(2,1)} %get-tuple-element.154, s32[1024]{0:T(1024)S(1)} %pad_clamp_fusion.2), kind=kCustom, calls=%fused_computation.clone.1 | custom fusion | bytes 10617048 | tf_op jit(solution)/shard_map/while/body/eval_jaxpr/gather | solution.py:103
  507.8 14.8 %fusion.47 = (f32[2,384]{1,0:T(2,128)S(1)}, f32[2,384,10368]{2,1,0:T(8,128)}) fusion(pred[2,10368]{1,0:T(4,128)(4,1)S(1)} %bitcast.96, bf16[2,10368,128]{2,1,0:T(8,128)(2,1)} %bitcast.86, bf16[3,2,384,128]{3,2,1,0:T(8,128)(2,1)} %get-tuple-element.152, s32[]{:T(128)} %get-tuple-element.141), kind=kOutput, calls=%fused_computation.4.clone.1 | convolution fusion | flops 2062318848 | bytes 37379840 | tf_op jit(solution)/shard_map/while/body/eval_jaxpr/jxg,jog->jxo/dot_general | solution.py:26
  522.6 14.3 %fusion.48 = f32[2,384]{1,0:T(2,128)S(1)} fusion(f32[2,384,10368]{2,1,0:T(8,128)} %get-tuple-element.131, f32[2,384]{1,0:T(2,128)S(1)} %get-tuple-element.132, pred[2,10368]{1,0:T(4,128)(4,1)S(1)} %bitcast.97), kind=kLoop, calls=%fused_computation.5.clone.1 | loop fusion | flops 31849728 | bytes 31877376 | tf_op jit(solution)/shard_map/while/body/eval_jaxpr/reduce_sum | solution.py:33
  536.9 7.7 %gather_fusion = bf16[54,384,128]{2,1,0:T(8,128)(2,1)} fusion(bf16[108,384,128]{2,1,0:T(8,128)(2,1)} %get-tuple-element.155, s32[1024]{0:T(1024)S(1)} %pad_clamp_fusion.2), kind=kCustom, calls=%fused_computation.1.clone.1 | custom fusion | bytes 10617048 | tf_op jit(solution)/shard_map/while/body/eval_jaxpr/gather | solution.py:103
  544.6 15.4 %fusion.49 = bf16[3,2,384,128]{3,2,1,0:T(8,128)(2,1)S(1)} fusion(bf16[3,2,384,128]{3,2,1,0:T(8,128)(2,1)S(1)} %get-tuple-element.142, s32[]{:T(128)} %get-tuple-element.141, bf16[2,10368,128]{2,1,0:T(8,128)(2,1)} %bitcast.87, f32[2,384,10368]{2,1,0:T(8,128)} %get-tuple-element.131, f32[2,384]{1,0:T(2,128)S(1)} %get-tuple-element.132, ...), kind=kOutput, calls=%fused_computation.12.clone.1 | convolution fusion | flops 2070478848 | bytes 37403140 | tf_op jit(solution)/shard_map/while/body/eval_jaxpr/aop,ape->aoe/dot_general | solution.py:34
  560.1 7.7 %gather_fusion.1 = bf16[54,384,128]{2,1,0:T(8,128)(2,1)} fusion(bf16[108,384,128]{2,1,0:T(8,128)(2,1)} %get-tuple-element.154, s32[1024]{0:T(1024)S(1)} %pad_clamp_fusion.2), kind=kCustom, calls=%fused_computation.clone.1 | custom fusion | bytes 10617048 | tf_op jit(solution)/shard_map/while/body/eval_jaxpr/gather | solution.py:103
  567.9 14.8 %fusion.47 = (f32[2,384]{1,0:T(2,128)S(1)}, f32[2,384,10368]{2,1,0:T(8,128)}) fusion(pred[2,10368]{1,0:T(4,128)(4,1)S(1)} %bitcast.96, bf16[2,10368,128]{2,1,0:T(8,128)(2,1)} %bitcast.86, bf16[3,2,384,128]{3,2,1,0:T(8,128)(2,1)} %get-tuple-element.152, s32[]{:T(128)} %get-tuple-element.141), kind=kOutput, calls=%fused_computation.4.clone.1 | convolution fusion | flops 2062318848 | bytes 37379840 | tf_op jit(solution)/shard_map/while/body/eval_jaxpr/jxg,jog->jxo/dot_general | solution.py:26
  582.7 14.3 %fusion.48 = f32[2,384]{1,0:T(2,128)S(1)} fusion(f32[2,384,10368]{2,1,0:T(8,128)} %get-tuple-element.131, f32[2,384]{1,0:T(2,128)S(1)} %get-tuple-element.132, pred[2,10368]{1,0:T(4,128)(4,1)S(1)} %bitcast.97), kind=kLoop, calls=%fused_computation.5.clone.1 | loop fusion | flops 31849728 | bytes 31877376 | tf_op jit(solution)/shard_map/while/body/eval_jaxpr/reduce_sum | solution.py:33
  597.0 7.7 %gather_fusion = bf16[54,384,128]{2,1,0:T(8,128)(2,1)} fusion(bf16[108,384,128]{2,1,0:T(8,128)(2,1)} %get-tuple-element.155, s32[1024]{0:T(1024)S(1)} %pad_clamp_fusion.2), kind=kCustom, calls=%fused_computation.1.clone.1 | custom fusion | bytes 10617048 | tf_op jit(solution)/shard_map/while/body/eval_jaxpr/gather | solution.py:103
  604.7 15.4 %fusion.49 = bf16[3,2,384,128]{3,2,1,0:T(8,128)(2,1)S(1)} fusion(bf16[3,2,384,128]{3,2,1,0:T(8,128)(2,1)S(1)} %get-tuple-element.142, s32[]{:T(128)} %get-tuple-element.141, bf16[2,10368,128]{2,1,0:T(8,128)(2,1)} %bitcast.87, f32[2,384,10368]{2,1,0:T(8,128)} %get-tuple-element.131, f32[2,384]{1,0:T(2,128)S(1)} %get-tuple-element.132, ...), kind=kOutput, calls=%fused_computation.12.clone.1 | convolution fusion | flops 2070478848 | bytes 37403140 | tf_op jit(solution)/shard_map/while/body/eval_jaxpr/aop,ape->aoe/dot_general | solution.py:34
  621.2 11.9 %all_to_all.25 = bf16[4,192,384]{2,1,0:T(8,128)(2,1)S(1)} all-to-all(bf16[4,192,384]{2,1,0:T(8,128)(2,1)S(1)} %all_to_all.18), channel_id=1, replica_groups=mesh['seq'=64,'head'=4] {'head'}, dimensions={0} | all-to-all | bytes 1179648 | tf_op jit(solution)/shard_map/all_to_all | solution.py:109
  (57 shorter events, 39.1 us)
Async XLA Ops:
  26.5 1.2 copy-start.3
  29.5 28.0 %collective-permute-start.1 = (bf16[2,3,2,384,128]{4,3,2,1,0:T(8,128)(2,1)}, bf16[2,3,2,384,128]{4,3,2,1,0:T(8,128)(2,1)}, u32[]{:S(2)}, u32[]{:S(2)}) collective-permute-start(bf16[2,3,2,384,128]{4,3,2,1,0:T(8,128)(2,1)} %copy.22), channel_id=1, source_target_pairs={{32,0},{36,4},{40,8},{44,12},{48,16},{52,20},{56,24},{60,28},{64,3... | collective-permute-start | bytes 3538952 | tf_op jit(solution)/shard_map/ppermute | solution.py:13
  33.1 53.3 %collective-permute-start = (bf16[2,3,2,384,128]{4,3,2,1,0:T(8,128)(2,1)}, bf16[2,3,2,384,128]{4,3,2,1,0:T(8,128)(2,1)}, u32[]{:S(2)}, u32[]{:S(2)}) collective-permute-start(bf16[2,3,2,384,128]{4,3,2,1,0:T(8,128)(2,1)} %copy.22), channel_id=1, source_target_pairs={{0,32},{4,36},{8,40},{12,44},{16,48},{20,52},{24,56},{28,60},{32,6... | collective-permute-start | bytes 3538952 | tf_op jit(solution)/shard_map/ppermute | solution.py:13
  88.6 89.5 %copy-start.1 = (bf16[2,3,2,384,128]{4,1,3,2,0:T(4,128)(2,1)}, bf16[2,3,2,384,128]{4,1,3,2,0:T(4,128)(2,1)S(1)}, u32[]{:S(2)}) copy-start(bf16[2,3,2,384,128]{4,1,3,2,0:T(4,128)(2,1)S(1)} %copy.48) | copy-start | bytes 3538948
  94.2 82.4 %collective-permute-start.2 = (bf16[2,3,3,384,128]{4,3,2,1,0:T(8,128)(2,1)S(1)}, bf16[2,3,3,384,128]{4,3,2,1,0:T(8,128)(2,1)S(1)}, u32[]{:S(2)}, u32[]{:S(2)}) collective-permute-start(bf16[2,3,3,384,128]{4,3,2,1,0:T(8,128)(2,1)S(1)} %copy.26), channel_id=1, source_target_pairs={{0,16},{4,20},{8,24},{12,28},{16,0},{20,4},{24,8},{28,12},{32,48},... | collective-permute-start | bytes 5308424 | tf_op jit(solution)/shard_map/ppermute | solution.py:19
  178.1 1.5 copy-start.2
  189.0 14.6 %copy-start.5 = (s32[3,2,27]{2,1,0:T(2,128)S(1)}, s32[3,2,27]{2,1,0:T(2,128)}, u32[]{:S(2)}) copy-start(s32[3,2,27]{2,1,0:T(2,128)} %param.5) | copy-start | bytes 1948
  197.5 154.9 %collective-permute-start.4 = (bf16[2,3,3,4,384,128]{5,4,3,2,1,0:T(8,128)(2,1)}, bf16[2,3,3,4,384,128]{5,4,3,2,1,0:T(8,128)(2,1)}, u32[]{:S(2)}, u32[]{:S(2)}) collective-permute-start(bf16[2,3,3,4,384,128]{5,4,3,2,1,0:T(8,128)(2,1)} %copy.28), channel_id=1, source_target_pairs={{4,0},{8,4},{12,8},{16,12},{20,16},{24,20},{28,24},{32,28},{36,32}... | collective-permute-start | bytes 21233672 | tf_op jit(solution)/shard_map/ppermute | solution.py:13
  199.4 163.3 %collective-permute-start.3 = (bf16[2,3,3,4,384,128]{5,4,3,2,1,0:T(8,128)(2,1)}, bf16[2,3,3,4,384,128]{5,4,3,2,1,0:T(8,128)(2,1)}, u32[]{:S(2)}, u32[]{:S(2)}) collective-permute-start(bf16[2,3,3,4,384,128]{5,4,3,2,1,0:T(8,128)(2,1)} %copy.28), channel_id=1, source_target_pairs={{0,4},{4,8},{8,12},{12,16},{16,20},{20,24},{24,28},{28,32},{32,36}... | collective-permute-start | bytes 21233672 | tf_op jit(solution)/shard_map/ppermute | solution.py:13
  420.9 13.1 %copy-start = (bf16[1,3,3,3,4,384,128]{6,1,5,4,0,3,2:T(4,128)(2,1)S(1)}, bf16[1,3,3,3,4,384,128]{6,1,5,4,0,3,2:T(4,128)(2,1)}, u32[]{:S(2)}) copy-start(bf16[1,3,3,3,4,384,128]{6,1,5,4,0,3,2:T(4,128)(2,1)} %get-tuple-element.80) | copy-start | bytes 31850500
  434.0 5.8 copy-start.4
